TPU v7x, 512 devices: a whole 4x8x8 slice. The times are simulated.
512 devices in a mesh: seq: 32 (over y, x), head: 16 (over z, core).
Axes of the slice: x: 4, y: 8, z: 8, core: 2. Of those that a mesh axis runs over, the one named last changes fastest.
Arguments:
- queries: bfloat16 [8192, 8192], P('seq', 'head'), may hold values from -1.796875 to 1.796875
- key_rows: bfloat16 [8192, 8192], P('seq', 'head'), may hold values from -1.796875 to 1.796875
- value_rows: bfloat16 [8192, 8192], P('seq', 'head'), may hold values from -6 to 6
- level_table: float32 [64, 7, 64], P(None, None, 'head'), may hold values from 0.25 to 4
- level_index: int32 [8192, 7], P('seq'), may hold values from 0 to 63
- norm_gain: float32 [8192], replicated, may hold values from 0.5 to 1.5
- cotangent: bfloat16 [8192, 8192], P(('seq', 'head')), may hold values from -6 to 6
Outputs:
- normed: bfloat16 [8192, 8192], P(('seq', 'head'))
- grad_query: bfloat16 [8192, 8192], P('seq', 'head')
- grad_key: bfloat16 [8192, 8192], P('seq', 'head')
- grad_value: bfloat16 [8192, 8192], P('seq', 'head')
- grad_table: float32 [64, 7, 64], P(None, None, 'head')
- grad_gain: float32 [8192], replicated
All inputs are finite; a program needn't handle non-finite values.
Results may differ from a plain program's by a relative error of at most 0.014.
Values may be sent and summed in bfloat16 or wider, within the bound.
A program may use at most 64 MiB of HBM per device.

v0:
```python
import jax
import jax.numpy as jnp
from jax import lax
from jax.sharding import PartitionSpec as P

CH = 128
LEVELS = 7
TABLE = 64
EPSILON = 1e-06
HIGHEST = lax.Precision.HIGHEST


def swapped(value, axis, bit):
    mask = 2**bit
    pairs = [(source, source ^ mask) for source in range(lax.axis_size(axis))]
    return lax.ppermute(value, axis, pairs)


def bit_length_of(values, places):
    result = jnp.zeros_like(values)
    for exponent in range(places):
        result = result + (values >= 1 << exponent).astype(jnp.int32)
    return result


def level_mask(spans):
    row_ids = lax.broadcasted_iota(jnp.int32, (spans, spans), 0)
    col_ids = lax.broadcasted_iota(jnp.int32, (spans, spans), 1)
    lengths = bit_length_of(jnp.bitwise_xor(row_ids, col_ids), 16)
    stacked = [((lengths == 1) & (col_ids < row_ids)).astype(jnp.float32)]
    return jnp.stack(stacked)


def body(queries, key_rows, value_rows, level_table, level_index, norm_gain, cotangent):
    tok_dev = queries.shape[0]
    head_count = level_table.shape[2]
    head_width = queries.shape[1] // head_count
    spans = tok_dev // CH
    local_bits = spans.bit_length() - 1
    seq_bits = lax.axis_size("seq").bit_length() - 1
    cross_count = LEVELS - 1 - local_bits
    shard_id = lax.axis_index("seq")
    query_blocks = queries.reshape(spans, CH, head_count, head_width)
    key_blocks = key_rows.reshape(spans, CH, head_count, head_width)
    value_blocks = value_rows.reshape(spans, CH, head_count, head_width)
    onehot = (level_index[:, :, None] == jnp.arange(TABLE, dtype=jnp.int32)[None, None, :]).astype(
        jnp.float32
    )
    weights = jnp.einsum("tlx,xlh->tlh", onehot, level_table, precision=HIGHEST)
    weights = weights.reshape(spans, CH, LEVELS, head_count)
    span_states = jnp.einsum(
        "icha,ichb->ihab", key_blocks, value_blocks, preferred_element_type=jnp.float32
    )
    masks_local = level_mask(spans)
    intra_states = jnp.einsum("mij,jhab->imhab", masks_local, span_states, precision=HIGHEST)
    shard_total = jnp.sum(span_states, axis=0)
    state_zeros = jnp.zeros((cross_count, head_count, head_width, head_width), jnp.float32)
    shards_in = lax.all_gather(
        shard_total[None].astype(jnp.bfloat16), "seq", axis=0, tiled=True
    ).astype(jnp.float32)
    source = jnp.arange(shards_in.shape[0], dtype=jnp.int32)
    lengths = bit_length_of(jnp.bitwise_xor(source, shard_id), 16)
    slot_of = jnp.minimum(lengths + local_bits, LEVELS - 1) - local_bits - 1
    selector = (slot_of[:, None] == jnp.arange(cross_count, dtype=jnp.int32)[None, :]) & (
        source < shard_id
    )[:, None]
    cross_states = state_zeros + jnp.einsum(
        "sk,shab->khab", selector.astype(jnp.float32), shards_in, precision=HIGHEST
    )
    spread = jnp.broadcast_to(cross_states[None], (spans,) + cross_states.shape)
    level_states = jnp.concatenate([intra_states, spread], axis=1).astype(jnp.bfloat16)
    far_out = jnp.einsum(
        "icha,ilhab->iclhb", query_blocks, level_states, preferred_element_type=jnp.float32
    )
    row_ids = lax.broadcasted_iota(jnp.int32, (CH, CH), 0)
    col_ids = lax.broadcasted_iota(jnp.int32, (CH, CH), 1)
    causal = col_ids <= row_ids
    scores = jnp.einsum(
        "icha,inha->ihcn", query_blocks, key_blocks, preferred_element_type=jnp.float32
    )
    scores = jnp.where(causal, scores, 0.0)
    near_out = jnp.einsum(
        "ihcn,inhb->ichb",
        scores.astype(jnp.bfloat16),
        value_blocks,
        preferred_element_type=jnp.float32,
    )
    level_out = jnp.concatenate([near_out[:, :, None], far_out], axis=2)
    attn = jnp.sum(weights[..., None] * level_out, axis=2).astype(jnp.bfloat16)
    attn_rows = attn.reshape(tok_dev, head_count * head_width)
    token_attn = lax.all_to_all(attn_rows, "head", split_axis=0, concat_axis=1, tiled=True)
    attn_f = token_attn.astype(jnp.float32)
    inv_rms = lax.rsqrt(jnp.mean(attn_f * attn_f, axis=1, keepdims=True) + EPSILON)
    unit_rows = attn_f * inv_rms
    normed = (unit_rows * norm_gain).astype(jnp.bfloat16)
    grad_out = cotangent.astype(jnp.float32)
    scaled = grad_out * norm_gain
    grad_gain = lax.psum(jnp.sum(grad_out * unit_rows, axis=0), ("seq", "head"))
    grad_attn = (
        (scaled - unit_rows * jnp.mean(scaled * unit_rows, axis=1, keepdims=True)) * inv_rms
    ).astype(jnp.bfloat16)
    head_grad = lax.all_to_all(grad_attn, "head", split_axis=1, concat_axis=0, tiled=True)
    grad_blocks = head_grad.reshape(spans, CH, head_count, head_width)
    grad_f = grad_blocks.astype(jnp.float32)
    grad_weight = jnp.sum(level_out * grad_f[:, :, None], axis=4)
    along_values = jnp.einsum(
        "ichb,inhb->ihcn", grad_blocks, value_blocks, preferred_element_type=jnp.float32
    )
    first_weight = jnp.transpose(weights[:, :, 0, :], (0, 2, 1))[..., None]
    grad_scores = jnp.where(causal, along_values * first_weight, 0.0).astype(jnp.bfloat16)
    weighted_scores = jnp.where(causal, scores * first_weight, 0.0).astype(jnp.bfloat16)
    near_dq = jnp.einsum(
        "ihcn,inha->icha", grad_scores, key_blocks, preferred_element_type=jnp.float32
    )
    near_dk = jnp.einsum(
        "ihcn,icha->inha", grad_scores, query_blocks, preferred_element_type=jnp.float32
    )
    near_dv = jnp.einsum(
        "ihcn,ichb->inhb", weighted_scores, grad_blocks, preferred_element_type=jnp.float32
    )
    far_dq = jnp.einsum(
        "ichb,ilhab->iclha", grad_blocks, level_states, preferred_element_type=jnp.float32
    )
    grad_query = near_dq + jnp.sum(weights[:, :, 1:, :, None] * far_dq, axis=2)
    scaled_grad = (weights[:, :, 1:, :, None] * grad_f[:, :, None]).astype(jnp.bfloat16)
    query_grads = jnp.einsum(
        "icha,iclhb->ilhab", query_blocks, scaled_grad, preferred_element_type=jnp.float32
    )
    inner_grad = jnp.einsum(
        "mij,imhab->jhab", masks_local, query_grads[:, :local_bits], precision=HIGHEST
    )
    shard_grads = jnp.sum(query_grads[:, local_bits:], axis=0)
    cross_grad = jnp.zeros((head_count, head_width, head_width), jnp.float32)
    group_grads = shard_grads
    for bit_pos in range(seq_bits):
        partner = swapped(group_grads.astype(jnp.bfloat16), "seq", bit_pos).astype(
            group_grads.dtype
        )
        lower_half = 1.0 - jnp.bitwise_and(jnp.right_shift(shard_id, bit_pos), 1).astype(
            jnp.float32
        )
        level_slot = min(bit_pos, cross_count - 1)
        cross_grad = cross_grad + lower_half * partner[level_slot]
        group_grads = group_grads + partner
    key_state = (inner_grad + cross_grad[None]).astype(jnp.bfloat16)
    grad_key = near_dk + jnp.einsum(
        "jhab,jnhb->jnha", key_state, value_blocks, preferred_element_type=jnp.float32
    )
    grad_value = near_dv + jnp.einsum(
        "jhab,jnha->jnhb", key_state, key_blocks, preferred_element_type=jnp.float32
    )
    table_part = jnp.einsum(
        "tlx,tlh->xlh", onehot, grad_weight.reshape(tok_dev, LEVELS, head_count), precision=HIGHEST
    )
    grad_table = lax.psum(table_part, "seq")
    row_shape = (tok_dev, head_count * head_width)
    return (
        normed,
        grad_query.astype(jnp.bfloat16).reshape(row_shape),
        grad_key.astype(jnp.bfloat16).reshape(row_shape),
        grad_value.astype(jnp.bfloat16).reshape(row_shape),
        grad_table,
        grad_gain,
    )


def solution(mesh):
    placed = (
        P("seq", "head"),
        P("seq", "head"),
        P("seq", "head"),
        P(None, None, "head"),
        P("seq", None),
        P(),
        P(("seq", "head"), None),
    )
    return jax.shard_map(
        body,
        mesh=mesh,
        in_specs=placed,
        out_specs=(
            P(("seq", "head"), None),
            P("seq", "head"),
            P("seq", "head"),
            P("seq", "head"),
            P(None, None, "head"),
            P(),
        ),
        check_vma=False,
    )
```

profile of v0, /device:TPU:32, one launch (start us, length us, event | category | flops | bytes accessed | tf_op | source)
XLA Modules:
  0.0 519.8 jit_solution(9532326248119924726)
XLA Ops:
  7.2 1.1 reshape.150
  8.3 1.0 reshape.151
  9.3 0.9 fusion.135
  10.3 0.3 convolution_bitcast_fusion.6
  10.7 1.3 fusion.16
  12.0 0.2 copy.206
  12.3 0.3 convolution_select_fusion
  12.6 0.8 copy-done.5
  13.4 0.3 convolution_bitcast_fusion.5
  13.8 86.5 %all-gather.3.cloned.1.call-done = bf16[128,128,128]{2,1,0:T(8,128)(2,1)} async-done(((bf16[4,128,128]{2,1,0:T(8,128)(2,1)}), bf16[128,128,128]{2,1,0:T(8,128)(2,1)}) %all-gather.3.cloned.1.call-update) | async-done | bytes 4194320 | tf_op jit(solution)/shard_map/all_gather | solution.py:58
  100.3 4.5 fusion.5
  104.8 0.6 copy.205
  105.4 0.3 broadcast_in_dim.23
  105.8 1.0 copy-done.4
  106.8 0.6 convolution_bitcast_fusion.1
  107.4 1.7 copy-done.1
  109.1 0.5 multiply_reduce_fusion.1
  110.0 18.5 %all_to_all.26 = bf16[16,16,512]{2,1,0:T(8,128)(2,1)S(1)} all-to-all(bf16[16,16,512]{2,1,0:T(8,128)(2,1)S(1)} %convert_element_type.402), channel_id=1, replica_groups=mesh['seq'=32,'head'=16] {'head'}, dimensions={0} | all-to-all | bytes 524288 | tf_op jit(solution)/shard_map/all_to_all | solution.py:91
  128.8 0.4 fusion.22
  129.1 0.9 fusion.21
  130.0 0.7 copy.311
  130.7 3.5 all-to-all-start.1
  134.3 11.3 %all-to-all-done.1 = bf16[16,16,512]{2,0,1:T(8,128)(2,1)S(1)} async-done(((bf16[16,16,512]{2,0,1:T(8,128)(2,1)}), bf16[16,16,512]{2,0,1:T(8,128)(2,1)S(1)}, u32[]{:S(2)}, u32[]{:S(2)}) %all-to-all-start.1) | async-done | bytes 262176 | tf_op jit(solution)/shard_map/all_to_all | solution.py:102
  145.7 0.7 copy-done.10
  146.4 0.2 copy.224
  146.7 0.6 convolution_bitcast_fusion
  147.2 0.2 copy-done.8
  147.7 1.4 copy-done.3
  149.2 2.8 collective-permute-start
  152.0 16.3 %collective-permute-done = bf16[5,4,128,128]{2,3,0,1:T(8,128)(2,1)S(1)} collective-permute-done((bf16[5,4,128,128]{2,3,0,1:T(8,128)(2,1)S(1)}, bf16[5,4,128,128]{2,3,0,1:T(8,128)(2,1)S(1)}, u32[]{:S(2)}, u32[]{:S(2)}) %collective-permute-start) | collective-permute-done | bytes 655392 | tf_op jit(solution)/shard_map/ppermute | solution.py:16
  168.4 1.0 fusion.56
  169.4 4.0 collective-permute-start.1
  173.4 16.0 %collective-permute-done.1 = bf16[5,4,128,128]{2,3,0,1:T(8,128)(2,1)S(1)} collective-permute-done((bf16[5,4,128,128]{2,3,0,1:T(8,128)(2,1)}, bf16[5,4,128,128]{2,3,0,1:T(8,128)(2,1)S(1)}, u32[]{:S(2)}, u32[]{:S(2)}) %collective-permute-start.1) | collective-permute-done | bytes 655392 | tf_op jit(solution)/shard_map/ppermute | solution.py:16
  189.4 1.1 fusion.27
  190.5 4.0 collective-permute-start.2
  194.5 100.7 %psum.15 = f32[8192]{0:T(1024)} all-reduce(f32[8192]{0:T(1024)S(1)} %get-tuple-element.6), channel_id=1, replica_groups=mesh['seq'=32,'head'=16] {'seq','head'}, use_global_device_ids=true, to_apply=%region_9.10 | all-reduce | flops 8192 | bytes 65536 | tf_op jit(solution)/shard_map/psum | solution.py:98
  295.2 3.0 fusion.2
  298.2 2.0 copy.219
  300.3 1.3 fusion.11
  301.6 2.5 fusion.26
  304.0 2.5 collective-permute-start.3
  306.5 0.2 fusion.14
  306.8 0.2 copy.220
  307.0 0.7 copy.310
  307.7 0.6 multiply_reduce_fusion
  308.4 1.9 slice_bitcast_fusion
  310.3 2.0 copy.226
  312.3 25.5 %collective-permute-done.3 = bf16[5,4,128,128]{2,3,0,1:T(8,128)(2,1)} collective-permute-done((bf16[5,4,128,128]{2,3,0,1:T(8,128)(2,1)}, bf16[5,4,128,128]{2,3,0,1:T(8,128)(2,1)}, u32[]{:S(2)}, u32[]{:S(2)}) %collective-permute-start.3) | collective-permute-done | bytes 655392 | tf_op jit(solution)/shard_map/ppermute | solution.py:16
  337.8 2.6 add_convert_fusion
  340.4 4.2 collective-permute-start.4
  344.6 0.3 convolution_bitcast_fusion.7
  344.9 157.1 %psum.14 = f32[64,7,4]{0,2,1:T(4,128)} all-reduce(f32[64,7,4]{0,2,1:T(4,128)S(1)} %convolution_bitcast_fusion.7), channel_id=1, replica_groups=mesh['seq'=32,'head'=16] {'seq'}, use_global_device_ids=true, to_apply=%region_7.8 | all-reduce | flops 1792 | bytes 14336 | tf_op jit(solution)/shard_map/psum | solution.py:155
  502.0 2.1 fusion.61
  504.1 2.4 fusion.28
  506.8 1.2 convert_element_type.422
  508.0 1.2 convert_element_type.425
  509.2 1.1 fusion.31
  510.5 0.3 convolution_bitcast_fusion.2
  510.8 0.3 fusion.15
  511.1 0.3 copy-done.14
  511.4 0.3 fusion.13
  511.7 0.2 copy.231
  511.9 0.2 copy.235
  512.1 0.9 copy_bitcast_fusion
  (63 shorter events, 1.7 us)
Async XLA Ops:
  7.2 3.1 copy-start
  7.2 3.1 copy-start.19
  7.2 3.4 copy-start.17
  7.2 93.1 %all-gather.3.cloned.1.call-start = ((), (), s32[]{:S(2)}) async-start(), calls=%async_computation.2 | async-start | bytes 4325376 | tf_op jit(solution)/shard_map/all_gather | solution.py:58
  12.2 93.5 %copy-start.15 = (bf16[2,1,4,128,128]{3,4,1,2,0:T(8,128)(2,1)}, bf16[2,1,4,128,128]{3,4,1,2,0:T(8,128)(2,1)S(1)}, u32[]{:S(2)}) copy-start(bf16[2,1,4,128,128]{3,4,1,2,0:T(8,128)(2,1)S(1)} %copy.206) | copy-start | bytes 786436
  12.6 0.8 copy-start.5
  13.8 93.6 %copy-start.6 = (f32[2,128,1,4,128]{1,4,2,3,0:T(8,128)}, f32[2,128,1,4,128]{1,4,2,3,0:T(8,128)S(1)}, u32[]{:S(2)}) copy-start(f32[2,128,1,4,128]{1,4,2,3,0:T(8,128)S(1)} %convolution_bitcast_fusion.5) | copy-start | bytes 1572868
  105.8 1.0 copy-start.4
  107.4 1.7 copy-start.1
  109.8 18.9 %copy-start.16 = (bf16[16,8192]{1,0:T(8,128)(2,1)S(1)}, bf16[16,8192]{1,0:T(8,128)(2,1)}, u32[]{:S(2)}) copy-start(bf16[16,8192]{1,0:T(8,128)(2,1)} %param.13) | copy-start | bytes 786436
  109.9 18.9 %copy-start.18 = (f32[8192]{0:T(1024)S(1)}, f32[8192]{0:T(1024)}, u32[]{:S(2)}) copy-start(f32[8192]{0:T(1024)} %param.12) | copy-start | bytes 98308
  130.7 14.9 %all-to-all-start.1 = ((bf16[16,16,512]{2,0,1:T(8,128)(2,1)}), bf16[16,16,512]{2,0,1:T(8,128)(2,1)S(1)}, u32[]{:S(2)}, u32[]{:S(2)}) async-start(bf16[16,16,512]{2,0,1:T(8,128)(2,1)} %bitcast.93), calls=%async_computation.1 | async-start | bytes 524288 | tf_op jit(solution)/shard_map/all_to_all | solution.py:102
  145.7 0.7 copy-start.10
  146.6 0.8 copy-start.8
  147.5 1.6 copy-start.3
  149.2 19.2 %collective-permute-start = (bf16[5,4,128,128]{2,3,0,1:T(8,128)(2,1)S(1)}, bf16[5,4,128,128]{2,3,0,1:T(8,128)(2,1)S(1)}, u32[]{:S(2)}, u32[]{:S(2)}) collective-permute-start(bf16[5,4,128,128]{2,3,0,1:T(8,128)(2,1)S(1)} %convert_element_type.415), channel_id=1, source_target_pairs={{0,16},{16,0},{32,48},{48,32},{64,80},{80,64},{96,112},{112,96},{1... | collective-permute-start | bytes 1966088 | tf_op jit(solution)/shard_map/ppermute | solution.py:16
  169.4 20.0 %collective-permute-start.1 = (bf16[5,4,128,128]{2,3,0,1:T(8,128)(2,1)}, bf16[5,4,128,128]{2,3,0,1:T(8,128)(2,1)S(1)}, u32[]{:S(2)}, u32[]{:S(2)}) collective-permute-start(bf16[5,4,128,128]{2,3,0,1:T(8,128)(2,1)} %fusion.56), channel_id=1, source_target_pairs={{0,32},{16,48},{32,0},{48,16},{64,96},{80,112},{96,64},{112,80},{1... | collective-permute-start | bytes 1966088 | tf_op jit(solution)/shard_map/ppermute | solution.py:16
  190.5 111.1 %collective-permute-start.2 = (bf16[5,4,128,128]{2,3,0,1:T(8,128)(2,1)}, bf16[5,4,128,128]{2,3,0,1:T(8,128)(2,1)}, u32[]{:S(2)}, u32[]{:S(2)}) collective-permute-start(bf16[5,4,128,128]{2,3,0,1:T(8,128)(2,1)} %fusion.27), channel_id=1, source_target_pairs={{0,64},{16,80},{32,96},{48,112},{64,0},{80,16},{96,32},{112,48},{1... | collective-permute-start | bytes 1966088 | tf_op jit(solution)/shard_map/ppermute | solution.py:16
  301.5 5.0 copy-start.13
  301.6 5.0 copy-start.12
  301.6 6.1 %copy-start.2 = (f32[2,128,6,4,128]{1,4,2,3,0:T(8,128)S(1)}, f32[2,128,6,4,128]{1,4,2,3,0:T(8,128)}, u32[]{:S(2)}) copy-start(f32[2,128,6,4,128]{1,4,2,3,0:T(8,128)} %copy-done.1) | copy-start | bytes 9437188
  304.0 3.7 copy-start.7
  304.0 3.7 copy-start.9
  304.0 33.8 %collective-permute-start.3 = (bf16[5,4,128,128]{2,3,0,1:T(8,128)(2,1)}, bf16[5,4,128,128]{2,3,0,1:T(8,128)(2,1)}, u32[]{:S(2)}, u32[]{:S(2)}) collective-permute-start(bf16[5,4,128,128]{2,3,0,1:T(8,128)(2,1)} %fusion.26), channel_id=1, source_target_pairs={{0,128},{16,144},{32,160},{48,176},{64,192},{80,208},{96,224},{112... | collective-permute-start | bytes 1966088 | tf_op jit(solution)/shard_map/ppermute | solution.py:16
  340.4 168.8 %collective-permute-start.4 = (bf16[5,4,128,128]{2,3,0,1:T(8,128)(2,1)}, bf16[5,4,128,128]{2,3,0,1:T(8,128)(2,1)}, u32[]{:S(2)}, u32[]{:S(2)}) collective-permute-start(bf16[5,4,128,128]{2,3,0,1:T(8,128)(2,1)} %add_convert_fusion), channel_id=1, source_target_pairs={{0,256},{16,272},{32,288},{48,304},{64,320},{80,336},{96,352},{112... | collective-permute-start | bytes 1966088 | tf_op jit(solution)/shard_map/ppermute | solution.py:16
  509.2 1.5 copy-start.11
  510.4 1.0 copy-start.14
Sparse Core Ops, SparseCore 0:
  11.8 88.4 all-gather.2
where the time goes:
time: 521 us; the launch traced here: 520 us
  blocking collectives  276 us (53%)
  waiting for transfers between devices  156 us (30%)
  starting transfers between devices  21.1 us (4%)
  local copies, waits for them, and re-layouts  19.3 us (4%)
  matrix products  19 us (4%)
  between operations  14.6 us (3%)
  other arithmetic  13.9 us (3%)
    psum x1, blocking collectives, body(): grad_table = lax.psum(table_part, 'seq')  157 us
    psum x1, blocking collectives, body(): grad_gain = lax.psum(jnp.sum(grad_out * unit_rows, axis=0), ('seq', 'head'))  101 us
    all_gather x1, waiting for transfers between devices, body(): lax.all_gather(shard_total[None].astype(jnp.bfloat16), 'seq', axis=0, til...  86.5 us
    ppermute x5, waiting for transfers between devices, swapped(): return lax.ppermute(value, axis, pairs)  57.8 us
    all_to_all x1, blocking collectives, body(): lax.all_to_all(attn_rows, 'head', split_axis=0, concat_axis=1, tiled=True)  18.5 us
    ppermute x5, starting transfers between devices, swapped(): return lax.ppermute(value, axis, pairs)  17.5 us
    all_to_all x1, waiting for transfers between devices, body(): lax.all_to_all(grad_attn, 'head', split_axis=1, concat_axis=0, tiled=True)  11.3 us
  transfers between devices with their start and end apart: 7, of which 5 were waited for; matrix products, arithmetic and copies ran while one was open for 4% of the time, Pallas kernels for 0%

commit v1 on v0

--- a/solution.py
+++ b/solution.py
@@ -1,3 +1,4 @@
+import functools
 import jax
 import jax.numpy as jnp
 from jax import lax
@@ -8,6 +9,14 @@
 TABLE = 64
 EPSILON = 1e-06
 HIGHEST = lax.Precision.HIGHEST
+
+
+def save_the_cells(inp, lane_axis, mesh_name):
+    z2 = jax.lax.psum(jax.lax.psum(inp, lane_axis), mesh_name)
+    return z2
+
+
+point_ports = functools.partial(save_the_cells, lane_axis="seq", mesh_name="head")
 
 
 def swapped(value, axis, bit):
@@ -95,7 +104,7 @@
     normed = (unit_rows * norm_gain).astype(jnp.bfloat16)
     grad_out = cotangent.astype(jnp.float32)
     scaled = grad_out * norm_gain
-    grad_gain = lax.psum(jnp.sum(grad_out * unit_rows, axis=0), ("seq", "head"))
+    grad_gain = point_ports(jnp.sum(grad_out * unit_rows, axis=0))
     grad_attn = (
         (scaled - unit_rows * jnp.mean(scaled * unit_rows, axis=1, keepdims=True)) * inv_rms
     ).astype(jnp.bfloat16)

time: 521 us -> 470 us (0.902)
  blocking collectives: 276 us -> 220 us
  waiting for transfers between devices: 156 us -> 163 us
    psum x1, blocking collectives: 101 us -> 46.3 us  [save_the_cells(): z2 = jax.lax.psum(jax.lax.psum(inp, lane_axis), mesh_name)]
    ppermute x5, waiting for transfers between devices: 57.8 us -> 64.9 us  [swapped(): return lax.ppermute(value, axis, pairs)]
  transfers between devices with their start and end apart: 7 -> 7, of which waited for: 5 -> 6; matrix products, arithmetic and copies ran while one was open for 4% -> 4% of each run, Pallas kernels for 0% -> 0%
where the time goes in v1:
time: 470 us; the launch traced here: 469 us
  blocking collectives  220 us (47%)
  waiting for transfers between devices  163 us (35%)
  starting transfers between devices  23.4 us (5%)
  local copies, waits for them, and re-layouts  19.5 us (4%)
  matrix products  15.5 us (3%)
  between operations  14.7 us (3%)
  other arithmetic  14.1 us (3%)
    psum x1, blocking collectives, body(): grad_table = lax.psum(table_part, 'seq')  155 us
    all_gather x1, waiting for transfers between devices, body(): lax.all_gather(shard_total[None].astype(jnp.bfloat16), 'seq', axis=0, til...  86.5 us
    ppermute x5, waiting for transfers between devices, swapped(): return lax.ppermute(value, axis, pairs)  64.9 us
    psum x1, blocking collectives, save_the_cells(): z2 = jax.lax.psum(jax.lax.psum(inp, lane_axis), mesh_name)  46.3 us
    ppermute x5, starting transfers between devices, swapped(): return lax.ppermute(value, axis, pairs)  19.8 us
    all_to_all x1, blocking collectives, body(): lax.all_to_all(attn_rows, 'head', split_axis=0, concat_axis=1, tiled=True)  18.5 us
    all_to_all x1, waiting for transfers between devices, body(): lax.all_to_all(grad_attn, 'head', split_axis=1, concat_axis=0, tiled=True)  11.3 us
  transfers between devices with their start and end apart: 7, of which 6 were waited for; matrix products, arithmetic and copies ran while one was open for 4% of the time, Pallas kernels for 0%

profile of v1, /device:TPU:32, one launch (start us, length us, event | category | flops | bytes accessed | tf_op | source)
XLA Modules:
  0.0 469.5 jit_solution(18112285213449288374)
XLA Ops:
  7.2 1.1 reshape.150
  8.3 1.0 reshape.151
  9.3 0.9 fusion.135
  10.3 0.3 convolution_bitcast_fusion.6
  10.7 1.3 fusion.16
  12.0 0.2 copy.206
  12.3 0.3 convolution_select_fusion
  12.6 0.8 copy-done.5
  13.5 0.3 convolution_bitcast_fusion.5
  13.8 86.5 %all-gather.3.cloned.1.call-done = bf16[128,128,128]{2,1,0:T(8,128)(2,1)} async-done(((bf16[4,128,128]{2,1,0:T(8,128)(2,1)}), bf16[128,128,128]{2,1,0:T(8,128)(2,1)}) %all-gather.3.cloned.1.call-update) | async-done | bytes 4194320 | tf_op jit(solution)/shard_map/all_gather | solution.py:67
  100.3 4.5 fusion.5
  104.8 0.6 copy.205
  105.4 0.3 broadcast_in_dim.23
  105.8 1.0 copy-done.3
  106.8 0.6 convolution_bitcast_fusion.1
  107.4 1.7 copy-done.1
  109.1 0.5 multiply_reduce_fusion.1
  110.0 18.5 %all_to_all.26 = bf16[16,16,512]{2,1,0:T(8,128)(2,1)S(1)} all-to-all(bf16[16,16,512]{2,1,0:T(8,128)(2,1)S(1)} %convert_element_type.402), channel_id=1, replica_groups=mesh['seq'=32,'head'=16] {'head'}, dimensions={0} | all-to-all | bytes 524288 | tf_op jit(solution)/shard_map/all_to_all | solution.py:100
  128.7 0.4 fusion.22
  129.1 0.9 fusion.21
  130.0 0.7 copy.311
  130.7 3.5 all-to-all-start.1
  134.3 11.3 %all-to-all-done.1 = bf16[16,16,512]{2,0,1:T(8,128)(2,1)S(1)} async-done(((bf16[16,16,512]{2,0,1:T(8,128)(2,1)}), bf16[16,16,512]{2,0,1:T(8,128)(2,1)S(1)}, u32[]{:S(2)}, u32[]{:S(2)}) %all-to-all-start.1) | async-done | bytes 262176 | tf_op jit(solution)/shard_map/all_to_all | solution.py:111
  145.7 0.7 copy-done.11
  146.4 0.2 copy.224
  146.6 0.6 convolution_bitcast_fusion
  147.2 0.2 copy-done.8
  147.6 1.4 copy-done.2
  149.2 2.8 collective-permute-start
  152.0 16.3 %collective-permute-done = bf16[5,4,128,128]{2,3,0,1:T(8,128)(2,1)S(1)} collective-permute-done((bf16[5,4,128,128]{2,3,0,1:T(8,128)(2,1)S(1)}, bf16[5,4,128,128]{2,3,0,1:T(8,128)(2,1)S(1)}, u32[]{:S(2)}, u32[]{:S(2)}) %collective-permute-start) | collective-permute-done | bytes 655392 | tf_op jit(solution)/shard_map/ppermute | solution.py:25
  168.3 1.1 fusion.56
  169.4 4.0 collective-permute-start.1
  173.5 15.9 %collective-permute-done.1 = bf16[5,4,128,128]{2,3,0,1:T(8,128)(2,1)S(1)} collective-permute-done((bf16[5,4,128,128]{2,3,0,1:T(8,128)(2,1)}, bf16[5,4,128,128]{2,3,0,1:T(8,128)(2,1)S(1)}, u32[]{:S(2)}, u32[]{:S(2)}) %collective-permute-start.1) | collective-permute-done | bytes 655392 | tf_op jit(solution)/shard_map/ppermute | solution.py:25
  189.4 1.2 fusion.27
  190.5 4.2 collective-permute-start.2
  194.8 1.6 fusion.2
  196.4 2.1 copy.219
  198.4 2.7 multiply_reduce_fusion
  201.2 7.4 %collective-permute-done.2 = bf16[5,4,128,128]{2,3,0,1:T(8,128)(2,1)} collective-permute-done((bf16[5,4,128,128]{2,3,0,1:T(8,128)(2,1)}, bf16[5,4,128,128]{2,3,0,1:T(8,128)(2,1)}, u32[]{:S(2)}, u32[]{:S(2)}) %collective-permute-start.2) | collective-permute-done | bytes 655392 | tf_op jit(solution)/shard_map/ppermute | solution.py:25
  208.6 1.4 fusion.26
  210.1 4.0 collective-permute-start.3
  214.1 0.3 fusion.11
  214.4 2.0 slice_bitcast_fusion
  216.5 0.2 fusion.14
  216.7 25.2 %collective-permute-done.3 = bf16[5,4,128,128]{2,3,0,1:T(8,128)(2,1)S(1)} collective-permute-done((bf16[5,4,128,128]{2,3,0,1:T(8,128)(2,1)S(1)}, bf16[5,4,128,128]{2,3,0,1:T(8,128)(2,1)S(1)}, u32[]{:S(2)}, u32[]{:S(2)}) %collective-permute-start.3) | collective-permute-done | bytes 655392 | tf_op jit(solution)/shard_map/ppermute | solution.py:25
  241.9 2.7 add_convert_fusion
  244.6 4.8 %collective-permute-start.4 = (bf16[5,4,128,128]{2,3,0,1:T(8,128)(2,1)}, bf16[5,4,128,128]{2,3,0,1:T(8,128)(2,1)}, u32[]{:S(2)}, u32[]{:S(2)}) collective-permute-start(bf16[5,4,128,128]{2,3,0,1:T(8,128)(2,1)} %add_convert_fusion), channel_id=1, source_target_pairs={{0,256},{16,272},{32,288},{48,304},{64,320},{80,336},{96,352},{112... | collective-permute-start | bytes 1966088 | tf_op jit(solution)/shard_map/ppermute | solution.py:25
  249.4 0.3 convolution_bitcast_fusion.7
  249.7 0.2 copy.220
  249.9 0.7 copy.310
  250.7 2.0 copy.226
  252.7 154.9 %all-reduce = (f32[64,7,4]{0,2,1:T(4,128)}, f32[8192]{0:T(1024)S(1)}) all-reduce(f32[64,7,4]{0,2,1:T(4,128)S(1)} %convolution_bitcast_fusion.7, f32[8192]{0:T(1024)S(1)} %get-tuple-element.6), channel_id=1, replica_groups=mesh['seq'=32,'head'=16] {'seq'}, use_global_device_ids=true, to_apply=%region_7.8 | all-reduce | flops 9984 | bytes 79872 | tf_op jit(solution)/shard_map/psum | solution.py:164
  407.6 46.3 %psum.23 = f32[8192]{0:T(1024)} all-reduce(f32[8192]{0:T(1024)S(1)} %get-tuple-element.9), channel_id=1, replica_groups=mesh['seq'=32,'head'=16] {'head'}, use_global_device_ids=true, to_apply=%region_10.11 | all-reduce | flops 8192 | bytes 65536 | tf_op jit(solution)/shard_map/psum | solution.py:15
  453.8 2.1 fusion.61
  456.0 1.2 fusion.28
  457.5 1.3 convert_element_type.422
  458.9 1.1 fusion.31
  460.1 0.3 convolution_bitcast_fusion.2
  460.4 0.3 fusion.15
  460.8 0.3 copy-done.18
  461.1 0.3 fusion.13
  461.4 0.2 copy.231
  461.6 0.2 copy.235
  461.8 0.9 copy_bitcast_fusion
  (73 shorter events, 1.9 us)
Async XLA Ops:
  7.2 3.1 copy-start
  7.2 3.1 copy-start.24
  7.2 3.4 copy-start.22
  7.2 93.1 %all-gather.3.cloned.1.call-start = ((), (), s32[]{:S(2)}) async-start(), calls=%async_computation.2 | async-start | bytes 4325376 | tf_op jit(solution)/shard_map/all_gather | solution.py:67
  12.2 93.5 %copy-start.19 = (bf16[2,1,4,128,128]{3,4,1,2,0:T(8,128)(2,1)}, bf16[2,1,4,128,128]{3,4,1,2,0:T(8,128)(2,1)S(1)}, u32[]{:S(2)}) copy-start(bf16[2,1,4,128,128]{3,4,1,2,0:T(8,128)(2,1)S(1)} %copy.206) | copy-start | bytes 786436
  12.6 0.9 copy-start.5
  13.8 93.6 %copy-start.7 = (f32[2,128,1,4,128]{1,4,2,3,0:T(8,128)}, f32[2,128,1,4,128]{1,4,2,3,0:T(8,128)S(1)}, u32[]{:S(2)}) copy-start(f32[2,128,1,4,128]{1,4,2,3,0:T(8,128)S(1)} %convolution_bitcast_fusion.5) | copy-start | bytes 1572868
  105.8 1.1 copy-start.3
  107.4 1.7 copy-start.1
  109.8 18.9 %copy-start.21 = (bf16[16,8192]{1,0:T(8,128)(2,1)S(1)}, bf16[16,8192]{1,0:T(8,128)(2,1)}, u32[]{:S(2)}) copy-start(bf16[16,8192]{1,0:T(8,128)(2,1)} %param.13) | copy-start | bytes 786436
  109.8 18.9 %copy-start.23 = (f32[8192]{0:T(1024)S(1)}, f32[8192]{0:T(1024)}, u32[]{:S(2)}) copy-start(f32[8192]{0:T(1024)} %param.12) | copy-start | bytes 98308
  130.7 14.9 %all-to-all-start.1 = ((bf16[16,16,512]{2,0,1:T(8,128)(2,1)}), bf16[16,16,512]{2,0,1:T(8,128)(2,1)S(1)}, u32[]{:S(2)}, u32[]{:S(2)}) async-start(bf16[16,16,512]{2,0,1:T(8,128)(2,1)} %bitcast.93), calls=%async_computation.1 | async-start | bytes 524288 | tf_op jit(solution)/shard_map/all_to_all | solution.py:111
  145.7 0.7 copy-start.11
  146.6 0.8 copy-start.8
  147.4 1.6 copy-start.2
  149.2 19.2 %collective-permute-start = (bf16[5,4,128,128]{2,3,0,1:T(8,128)(2,1)S(1)}, bf16[5,4,128,128]{2,3,0,1:T(8,128)(2,1)S(1)}, u32[]{:S(2)}, u32[]{:S(2)}) collective-permute-start(bf16[5,4,128,128]{2,3,0,1:T(8,128)(2,1)S(1)} %convert_element_type.415), channel_id=1, source_target_pairs={{0,16},{16,0},{32,48},{48,32},{64,80},{80,64},{96,112},{112,96},{1... | collective-permute-start | bytes 1966088 | tf_op jit(solution)/shard_map/ppermute | solution.py:25
  169.4 20.0 %collective-permute-start.1 = (bf16[5,4,128,128]{2,3,0,1:T(8,128)(2,1)}, bf16[5,4,128,128]{2,3,0,1:T(8,128)(2,1)S(1)}, u32[]{:S(2)}, u32[]{:S(2)}) collective-permute-start(bf16[5,4,128,128]{2,3,0,1:T(8,128)(2,1)} %fusion.56), channel_id=1, source_target_pairs={{0,32},{16,48},{32,0},{48,16},{64,96},{80,112},{96,64},{112,80},{1... | collective-permute-start | bytes 1966088 | tf_op jit(solution)/shard_map/ppermute | solution.py:25
  173.4 21.3 %copy-start.4 = (bf16[2,5,4,128,128]{3,4,1,2,0:T(8,128)(2,1)S(1)}, bf16[2,5,4,128,128]{3,4,1,2,0:T(8,128)(2,1)}, u32[]{:S(2)}) copy-start(bf16[2,5,4,128,128]{3,4,1,2,0:T(8,128)(2,1)} %copy-done.3) | copy-start | bytes 3932164
  173.4 21.3 %copy-start.12 = (bf16[2,128,4,128]{3,2,1,0:T(4,128)(2,1)S(1)}, bf16[2,128,4,128]{3,2,1,0:T(4,128)(2,1)}, u32[]{:S(2)}) copy-start(bf16[2,128,4,128]{3,2,1,0:T(4,128)(2,1)} %copy-done.11) | copy-start | bytes 786436
  173.5 21.3 %copy-start.20 = (bf16[2,1,4,128,128]{3,4,1,2,0:T(8,128)(2,1)S(1)}, bf16[2,1,4,128,128]{3,4,1,2,0:T(8,128)(2,1)}, u32[]{:S(2)}) copy-start(bf16[2,1,4,128,128]{3,4,1,2,0:T(8,128)(2,1)} %copy-done.19) | copy-start | bytes 786436
  190.5 18.1 %collective-permute-start.2 = (bf16[5,4,128,128]{2,3,0,1:T(8,128)(2,1)}, bf16[5,4,128,128]{2,3,0,1:T(8,128)(2,1)}, u32[]{:S(2)}, u32[]{:S(2)}) collective-permute-start(bf16[5,4,128,128]{2,3,0,1:T(8,128)(2,1)} %fusion.27), channel_id=1, source_target_pairs={{0,64},{16,80},{32,96},{48,112},{64,0},{80,16},{96,32},{112,48},{1... | collective-permute-start | bytes 1966088 | tf_op jit(solution)/shard_map/ppermute | solution.py:25
  201.2 12.9 %copy-start.13 = (bf16[2,128,4,128]{3,2,1,0:T(4,128)(2,1)S(1)}, bf16[2,128,4,128]{3,2,1,0:T(4,128)(2,1)}, u32[]{:S(2)}) copy-start(bf16[2,128,4,128]{3,2,1,0:T(4,128)(2,1)} %copy-done.11) | copy-start | bytes 786436
  210.1 6.4 %copy-start.16 = (f32[2,128,4,128]{3,1,2,0:T(8,128)S(1)}, f32[2,128,4,128]{3,1,2,0:T(8,128)}, u32[]{:S(2)}) copy-start(f32[2,128,4,128]{3,1,2,0:T(8,128)} %copy.219) | copy-start | bytes 1572868
  210.1 31.9 %collective-permute-start.3 = (bf16[5,4,128,128]{2,3,0,1:T(8,128)(2,1)S(1)}, bf16[5,4,128,128]{2,3,0,1:T(8,128)(2,1)S(1)}, u32[]{:S(2)}, u32[]{:S(2)}) collective-permute-start(bf16[5,4,128,128]{2,3,0,1:T(8,128)(2,1)S(1)} %fusion.26), channel_id=1, source_target_pairs={{0,128},{16,144},{32,160},{48,176},{64,192},{80,208},{96,224},{112... | collective-permute-start | bytes 1966088 | tf_op jit(solution)/shard_map/ppermute | solution.py:25
  214.4 2.3 copy-start.17
  241.9 2.7 copy-start.9
  244.6 214.3 %collective-permute-start.4 = (bf16[5,4,128,128]{2,3,0,1:T(8,128)(2,1)}, bf16[5,4,128,128]{2,3,0,1:T(8,128)(2,1)}, u32[]{:S(2)}, u32[]{:S(2)}) collective-permute-start(bf16[5,4,128,128]{2,3,0,1:T(8,128)(2,1)} %add_convert_fusion), channel_id=1, source_target_pairs={{0,256},{16,272},{32,288},{48,304},{64,320},{80,336},{96,352},{112... | collective-permute-start | bytes 1966088 | tf_op jit(solution)/shard_map/ppermute | solution.py:25
  249.7 206.3 %copy-start.6 = (f32[2,4,128,128]{3,2,1,0:T(8,128)S(1)}, f32[2,4,128,128]{3,2,1,0:T(8,128)}, u32[]{:S(2)}) copy-start(f32[2,4,128,128]{3,2,1,0:T(8,128)} %copy-done.5) | copy-start | bytes 1572868
  249.7 206.3 %copy-start.14 = (bf16[2,128,4,128]{3,2,1,0:T(4,128)(2,1)S(1)}, bf16[2,128,4,128]{3,2,1,0:T(4,128)(2,1)}, u32[]{:S(2)}) copy-start(bf16[2,128,4,128]{3,2,1,0:T(4,128)(2,1)} %copy-done.11) | copy-start | bytes 786436
  457.3 1.4 copy-start.10
  458.9 1.5 copy-start.15
  460.1 1.0 copy-start.18
Sparse Core Ops, SparseCore 0:
  11.8 88.4 all-gather.2
